TPU v7x, 128 devices: a whole 4x4x4 slice. The times are simulated.
128 devices in a mesh: tm: 64 (over x, z, y), head: 2 (over core).
Axes of the slice: x: 4, y: 4, z: 4, core: 2. Of those that a mesh axis runs over, the one named last changes fastest.
Arguments:
- series: bfloat16 [16, 65536, 512], P(None, 'tm'), may hold values from -6 to 6
- modes: int32 [128], replicated, may hold values from 1 to 32767, as said below
- query_weight: bfloat16 [512, 512], P(None, 'head'), may hold values from -0.25 to 0.25
- mix_weight: float32 [128, 8, 64, 128], P('tm', 'head'), may hold values from -0.5 to 0.5
- out_weight: bfloat16 [512, 512], P(None, 'head'), may hold values from -0.25 to 0.25
Outputs:
- output: bfloat16 [16, 65536, 512], P(None, 'tm', 'head')
Inputs may be any that keep to these rules, and one draw needn't show every extreme that they name: `modes`: distinct mode numbers; both 1 and one less than half of 65536 are among them.
All inputs are finite; a program needn't handle non-finite values.
Results may differ from a plain program's by a relative error of at most 0.0075.
Values may be sent and summed in bfloat16 or wider, within the bound.
A program may use at most 128 MiB of HBM per device.

v0:
```python
import math
import jax
import jax.numpy as jnp
from jax import lax
from jax.sharding import PartitionSpec as P

two_pi = 2.0 * math.pi


def wave_tables(mode_list, first_time, time_count, series_length):
    time_index = first_time + lax.iota(jnp.int32, time_count)
    phases = time_index[:, None] * mode_list[None, :] % series_length
    angles = phases.astype(jnp.float32) * (two_pi / series_length)
    return (jnp.cos(angles).astype(jnp.bfloat16), jnp.sin(angles).astype(jnp.bfloat16))


def body(series, modes, query_weight, mix_weight, out_weight):
    series_count, shard_rows, model_width = series.shape
    group_width = query_weight.shape[1]
    mode_total = modes.shape[0]
    own_modes = mix_weight.shape[0]
    heads_here = mix_weight.shape[1]
    head_size = mix_weight.shape[2]
    series_length = lax.axis_size("tm") * shard_rows
    first_time = lax.axis_index("tm") * shard_rows
    forward_scale = 1.0 / math.sqrt(series_length)
    inverse_scale = 1.0 / math.sqrt(mode_total)
    queries = jnp.dot(
        series.reshape(series_count * shard_rows, model_width),
        query_weight,
        preferred_element_type=jnp.float32,
    )
    queries = queries.astype(jnp.bfloat16).reshape(series_count, shard_rows, group_width)
    cosine, sine_part = wave_tables(modes, first_time, shard_rows, series_length)
    real_part = jnp.einsum("tm,btf->mbf", cosine, queries, preferred_element_type=jnp.float32)
    imag_part = jnp.einsum("tm,btf->mbf", sine_part, queries, preferred_element_type=jnp.float32)
    summed_all = lax.psum(jnp.stack([real_part, -imag_part], axis=1) * forward_scale, "tm")
    spectrum = lax.dynamic_slice_in_dim(summed_all, lax.axis_index("tm") * own_modes, own_modes, 0)
    spec_parts = spectrum.reshape(own_modes, 2, series_count, heads_here, head_size)
    from_real = jnp.einsum(
        "mbhi,mhio->mbho", spec_parts[:, 0], mix_weight, precision=lax.Precision.HIGHEST
    )
    from_imag = jnp.einsum(
        "mbhi,mhio->mbho", spec_parts[:, 1], mix_weight, precision=lax.Precision.HIGHEST
    )
    mixed_real = from_real[..., :head_size] - from_imag[..., head_size:]
    mixed_imag = from_real[..., head_size:] + from_imag[..., :head_size]
    mixed_spectra = jnp.stack([mixed_real, mixed_imag], axis=1).reshape(
        own_modes, 2, series_count, group_width
    )
    mixed_spectra = mixed_spectra.astype(jnp.bfloat16)
    cosine, sine_part = wave_tables(modes, first_time, shard_rows, series_length)
    wave_table = jnp.concatenate([cosine, -sine_part], axis=1)
    by_mode = lax.all_gather(mixed_spectra, "tm", axis=0, tiled=True)
    all_spectra = lax.all_gather(by_mode, "head", axis=3, tiled=True)
    stacked = jnp.concatenate([all_spectra[:, 0], all_spectra[:, 1]], axis=0)
    summed = jnp.einsum("tk,kbf->btf", wave_table, stacked, preferred_element_type=jnp.float32)
    restored = (summed * inverse_scale).astype(jnp.bfloat16)
    output = jnp.dot(
        restored.reshape(series_count * shard_rows, model_width),
        out_weight,
        preferred_element_type=jnp.float32,
    )
    return output.astype(jnp.bfloat16).reshape(series_count, shard_rows, group_width)


def solution(mesh):
    in_specs = (
        P(None, "tm", None),
        P(),
        P(None, "head"),
        P("tm", "head", None, None),
        P(None, "head"),
    )
    out_specs = P(None, "tm", "head")
    return jax.shard_map(body, mesh=mesh, in_specs=in_specs, out_specs=out_specs, check_vma=False)
```

profile of v0, /device:TPU:1, one launch (start us, length us, event | category | flops | bytes accessed | tf_op | source)
XLA Modules:
  0.0 306.4 jit_solution(206311727932910354)
XLA Ops:
  6.5 0.0 copy-start
  6.5 0.0 all-reduce.2.cloned.1.call-start
  6.5 0.9 copy-done
  7.5 0.0 copy-start.3
  7.5 10.3 %convolution_convert_fusion.1 = bf16[16384,256]{1,0:T(8,128)(2,1)S(1)} fusion(bf16[16384,512]{1,0:T(8,128)(2,1)} %bitcast.50, bf16[512,256]{1,0:T(8,128)(2,1)S(1)} %copy-done), kind=kOutput, calls=%fused_computation.2 | convolution fusion | flops 4299161600 | bytes 25427968 | tf_op jit(solution)/shard_map/dot_general | solution.py:28
  17.8 0.0 copy-done.3
  17.8 3.0 negate_bitcast_fusion
  20.8 3.0 convolution_bitcast_fusion
  23.8 2.4 maximum_multiply_fusion
  26.2 0.0 copy-start.2
  26.2 0.0 all-reduce.2.cloned.1.call-update
  26.3 0.0 all-gather.3.cloned.1.call-start
  26.3 140.7 %all-reduce.2.cloned.1.call-done = f32[128,2,16,256]{3,0,2,1:T(8,128)} async-done(((f32[128,2,16,256]{3,0,2,1:T(8,128)}), f32[128,2,16,256]{3,0,2,1:T(8,128)}) %all-reduce.2.cloned.1.call-update) | async-done | bytes 4194320 | tf_op jit(solution)/shard_map/psum | solution.py:37
  167.0 1.0 constant_dynamic-slice_fusion
  168.0 0.1 reshape.35
  168.1 0.0 copy-done.2
  168.1 0.3 convolution_bitcast_fusion.2
  168.5 0.3 convolution_bitcast_fusion.1
  168.8 0.1 fusion.13
  168.9 0.1 stack.21
  169.1 0.1 stack.22
  169.2 0.6 pad_maximum_fusion
  169.8 0.0 all-gather.3.cloned.1.call-update
  169.8 0.2 all-gather.5.cloned.1.call-start
  170.0 63.9 %all-gather.3.cloned.1.call-done = bf16[128,2,16,256]{3,2,1,0:T(8,128)(2,1)} async-done(((bf16[2,2,16,256]{3,2,1,0:T(8,128)(2,1)}), bf16[128,2,16,256]{3,2,1,0:T(8,128)(2,1)}) %all-gather.3.cloned.1.call-update) | async-done | bytes 2097168 | tf_op jit(solution)/shard_map/all_gather | solution.py:54
  233.9 4.5 %copy.27 = bf16[128,2,16,256]{0,3,2,1:T(8,128)(2,1)} copy(bf16[128,2,16,256]{3,2,1,0:T(8,128)(2,1)} %all-gather.3.cloned.1.call-done) | data formatting | bytes 4194304 | tf_op jit(solution)/shard_map/all_gather | solution.py:54
  238.4 0.0 all-gather.5.cloned.1.call-update
  238.4 2.3 fusion.11
  240.7 2.3 cosine_convert_fusion
  243.0 10.8 %all-gather.5.cloned.1.call-done = bf16[128,2,16,512]{0,3,2,1:T(8,128)(2,1)} async-done(((bf16[128,2,16,256]{0,3,2,1:T(8,128)(2,1)}), bf16[128,2,16,512]{0,3,2,1:T(8,128)(2,1)}) %all-gather.5.cloned.1.call-update) | async-done | bytes 4194320 | tf_op jit(solution)/shard_map/all_gather | solution.py:55
  253.8 2.5 slice_bitcast_fusion.1
  256.4 8.2 %fusion = bf16[16,1024,512]{1,2,0:T(8,128)(2,1)} fusion(bf16[128,16,512]{0,2,1:T(8,128)(2,1)S(1)} %get-tuple-element.6, bf16[128,16,512]{0,2,1:T(8,128)(2,1)S(1)} %get-tuple-element.5, bf16[1024,128]{1,0:T(8,128)(2,1)S(1)} %fusion.11, bf16[1024,128]{1,0:T(8,128)(2,1)S(1)} %cosine_convert_fusion), kind=kOutput, calls=%fused_computation.3 | convolution fusion | flops 4321181696 | bytes 21495808 | tf_op jit(solution)/shard_map/tk,kbf->btf/dot_general | solution.py:57
  264.5 0.0 copy-start.4
  264.5 21.7 %copy.28 = bf16[16,1024,512]{2,1,0:T(8,128)(2,1)} copy(bf16[16,1024,512]{1,2,0:T(8,128)(2,1)} %fusion) | data formatting | bytes 33554432 | tf_op jit(solution)/shard_map/convert_element_type | solution.py:58
  286.2 0.0 copy-done.4
  286.2 0.0 copy-start.1
  286.2 13.7 %convolution_convert_fusion = bf16[16384,256]{1,0:T(8,128)(2,1)} fusion(bf16[16384,512]{1,0:T(8,128)(2,1)} %bitcast.47, bf16[512,256]{1,0:T(8,128)(2,1)S(1)} %copy-done.4), kind=kOutput, calls=%fused_computation.1 | convolution fusion | flops 4299161600 | bytes 25427968 | tf_op jit(solution)/shard_map/dot_general | solution.py:59
  299.9 0.0 copy-done.1
  (4 shorter events, 0.0 us)
Async XLA Ops:
  6.5 1.0 copy-start
  6.5 160.4 %all-reduce.2.cloned.1.call-start = ((), (), s32[]{:S(2)}) async-start(), calls=%async_computation | async-start | bytes 8388608 | tf_op jit(solution)/shard_map/psum | solution.py:37
  7.5 10.3 %copy-start.3 = (s32[128]{0:T(128)S(1)}, s32[128]{0:T(128)}, u32[]{:S(2)}) copy-start(s32[128]{0:T(128)} %param.6) | copy-start | bytes 1540
  26.2 141.9 %copy-start.2 = (f32[2,4,64,128]{3,2,1,0:T(8,128)S(1)}, f32[2,4,64,128]{3,2,1,0:T(8,128)}, u32[]{:S(2)}) copy-start(f32[2,4,64,128]{3,2,1,0:T(8,128)} %param.8) | copy-start | bytes 786436
  26.3 207.6 %all-gather.3.cloned.1.call-start = ((), (), s32[]{:S(2)}) async-start(), calls=%async_computation.1 | async-start | bytes 2129920 | tf_op jit(solution)/shard_map/all_gather | solution.py:54
  169.8 84.0 %all-gather.5.cloned.1.call-start = ((), (), s32[]{:S(2)}) async-start(), calls=%async_computation.2 | async-start | bytes 6291456 | tf_op jit(solution)/shard_map/all_gather | solution.py:55
  264.5 21.7 %copy-start.4 = (bf16[512,256]{1,0:T(8,128)(2,1)S(1)}, bf16[512,256]{1,0:T(8,128)(2,1)}, u32[]{:S(2)}) copy-start(bf16[512,256]{1,0:T(8,128)(2,1)} %param.9) | copy-start | bytes 786436
  286.2 13.7 %copy-start.1 = (bf16[512,256]{1,0:T(8,128)(2,1)S(1)}, bf16[512,256]{1,0:T(8,128)(2,1)}, u32[]{:S(2)}) copy-start(bf16[512,256]{1,0:T(8,128)(2,1)} %param.7) | copy-start | bytes 786436
Sparse Core Ops, SparseCore 0:
  26.4 140.5 all-reduce.1
  170.3 63.6 all-gather.2
  238.6 15.2 all-gather.4
where the time goes:
time: 307 us; the launch traced here: 306 us
  waiting for transfers between devices  215 us (70%)
  matrix products  38.9 us (13%)
  local copies, waits for them, and re-layouts  31 us (10%)
  between operations  13.2 us (4%)
  other arithmetic  7.68 us (3%)
    psum x1, waiting for transfers between devices, body(): lax.psum(jnp.stack([real_part, -imag_part], axis=1) * forward_scale, 'tm')  141 us
    all_gather x1, waiting for transfers between devices, body(): by_mode = lax.all_gather(mixed_spectra, 'tm', axis=0, tiled=True)  63.9 us
    convert_element_type x1, local copies, waits for them, and re-layouts, body(): restored = (summed * inverse_scale).astype(jnp.bfloat16)  21.7 us
    dot_general x1, matrix products, body(): jnp.dot(restored.reshape(series_count * shard_rows, model_width), out_wei...  13.7 us
    all_gather x1, waiting for transfers between devices, body(): all_spectra = lax.all_gather(by_mode, 'head', axis=3, tiled=True)  10.8 us
    dot_general x1, matrix products, body(): jnp.dot(series.reshape(series_count * shard_rows, model_width), query_wei...  10.3 us
    dot_general x1, matrix products, body(): jnp.einsum('tk,kbf->btf', wave_table, stacked, preferred_element_type=jnp...  8.16 us
  transfers between devices with their start and end apart: 3, of which 3 were waited for; matrix products, arithmetic and copies ran while one was open for 1% of the time, Pallas kernels for 0%

commit v1 on v0

--- a/solution.py
+++ b/solution.py
@@ -52,7 +52,9 @@
     cosine, sine_part = wave_tables(modes, first_time, shard_rows, series_length)
     wave_table = jnp.concatenate([cosine, -sine_part], axis=1)
     by_mode = lax.all_gather(mixed_spectra, "tm", axis=0, tiled=True)
-    all_spectra = lax.all_gather(by_mode, "head", axis=3, tiled=True)
+    all_spectra = jnp.concatenate(
+        lax.all_to_all(jnp.stack([by_mode] * lax.axis_size("head")), "head", 0, 0), axis=3
+    )
     stacked = jnp.concatenate([all_spectra[:, 0], all_spectra[:, 1]], axis=0)
     summed = jnp.einsum("tk,kbf->btf", wave_table, stacked, preferred_element_type=jnp.float32)
     restored = (summed * inverse_scale).astype(jnp.bfloat16)

time: 307 us -> 308 us (level)
  waiting for transfers between devices: 215 us -> 199 us
  blocking collectives: 0 us -> 10.2 us
  local copies, waits for them, and re-layouts: 31 us -> 34.3 us
    all_gather x1 -> x0, waiting for transfers between devices: 10.8 us -> none  [body(): all_spectra = lax.all_gather(by_mode, 'head', axis=3, tiled=True)]
    all_to_all x0 -> x1, blocking collectives: none -> 10.2 us  [body(): lax.all_to_all(jnp.stack([by_mode] * lax.axis_size('head')), 'head', 0, 0)]
    reshape x0 -> x1, local copies, waits for them, and re-layouts: none -> 7.86 us  [body(): jnp.concatenate(lax.all_to_all(jnp.stack([by_mode] * lax.axis_size('head'...]
    all_gather x1, waiting for transfers between devices: 63.9 us -> 59 us  [body(): by_mode = lax.all_gather(mixed_spectra, 'tm', axis=0, tiled=True)]
    all_gather x1 -> x0, local copies, waits for them, and re-layouts: 4.51 us -> none  [body(): by_mode = lax.all_gather(mixed_spectra, 'tm', axis=0, tiled=True)]
  transfers between devices with their start and end apart: 3 -> 2, of which waited for: 3 -> 2; matrix products, arithmetic and copies ran while one was open for 1% -> 1% of each run, Pallas kernels for 0% -> 0%
where the time goes in v1:
time: 308 us; the launch traced here: 307 us
  waiting for transfers between devices  199 us (65%)
  matrix products  38.9 us (13%)
  local copies, waits for them, and re-layouts  34.3 us (11%)
  between operations  13.5 us (4%)
  other arithmetic  10.3 us (3%)
  blocking collectives  10.2 us (3%)
    psum x1, waiting for transfers between devices, body(): lax.psum(jnp.stack([real_part, -imag_part], axis=1) * forward_scale, 'tm')  140 us
    all_gather x1, waiting for transfers between devices, body(): by_mode = lax.all_gather(mixed_spectra, 'tm', axis=0, tiled=True)  59 us
    convert_element_type x1, local copies, waits for them, and re-layouts, body(): restored = (summed * inverse_scale).astype(jnp.bfloat16)  21.6 us
    dot_general x1, matrix products, body(): jnp.dot(restored.reshape(series_count * shard_rows, model_width), out_wei...  13.7 us
    dot_general x1, matrix products, body(): jnp.dot(series.reshape(series_count * shard_rows, model_width), query_wei...  10.3 us
    all_to_all x1, blocking collectives, body(): lax.all_to_all(jnp.stack([by_mode] * lax.axis_size('head')), 'head', 0, 0)  10.2 us
    dot_general x1, matrix products, body(): jnp.einsum('tk,kbf->btf', wave_table, stacked, preferred_element_type=jnp...  8.15 us
    reshape x1, local copies, waits for them, and re-layouts, body(): jnp.concatenate(lax.all_to_all(jnp.stack([by_mode] * lax.axis_size('head'...  7.86 us
  transfers between devices with their start and end apart: 2, of which 2 were waited for; matrix products, arithmetic and copies ran while one was open for 1% of the time, Pallas kernels for 0%

profile of v1, /device:TPU:1, one launch (start us, length us, event | category | flops | bytes accessed | tf_op | source)
XLA Modules:
  0.0 306.8 jit_solution(12860841057305628679)
XLA Ops:
  6.5 0.0 copy-start
  6.5 0.0 all-reduce.2.cloned.1.call-start
  6.5 0.9 copy-done
  7.5 0.0 copy-start.3
  7.5 10.3 %convolution_convert_fusion.1 = bf16[16384,256]{1,0:T(8,128)(2,1)S(1)} fusion(bf16[16384,512]{1,0:T(8,128)(2,1)} %bitcast.52, bf16[512,256]{1,0:T(8,128)(2,1)S(1)} %copy-done), kind=kOutput, calls=%fused_computation.2 | convolution fusion | flops 4299161600 | bytes 25427968 | tf_op jit(solution)/shard_map/dot_general | solution.py:28
  17.8 0.0 copy-done.3
  17.8 3.0 negate_bitcast_fusion
  20.8 3.0 convolution_bitcast_fusion
  23.8 2.4 maximum_multiply_fusion
  26.2 0.0 copy-start.2
  26.2 0.0 all-reduce.2.cloned.1.call-update
  26.3 0.2 all-gather.2.cloned.1.call-start
  26.5 140.5 %all-reduce.2.cloned.1.call-done = f32[128,2,16,256]{3,0,2,1:T(8,128)} async-done(((f32[128,2,16,256]{3,0,2,1:T(8,128)}), f32[128,2,16,256]{3,0,2,1:T(8,128)}) %all-reduce.2.cloned.1.call-update) | async-done | bytes 4194320 | tf_op jit(solution)/shard_map/psum | solution.py:37
  167.0 1.0 constant_dynamic-slice_fusion
  168.0 0.1 reshape.43
  168.1 0.0 copy-done.2
  168.1 0.3 convolution_bitcast_fusion.2
  168.5 0.3 convolution_bitcast_fusion.1
  168.8 0.1 fusion.13
  168.9 0.1 stack.28
  169.1 0.1 stack.29
  169.2 0.6 pad_maximum_fusion.1
  169.8 0.0 all-gather.2.cloned.1.call-update
  169.8 2.3 fusion.11
  172.1 2.3 cosine_convert_fusion
  174.4 59.0 %all-gather.2.cloned.1.call-done = bf16[128,2,16,256]{3,2,0,1:T(8,128)(2,1)} async-done(((bf16[2,2,16,256]{3,2,0,1:T(8,128)(2,1)}), bf16[128,2,16,256]{3,2,0,1:T(8,128)(2,1)}) %all-gather.2.cloned.1.call-update) | async-done | bytes 2097168 | tf_op jit(solution)/shard_map/all_gather | solution.py:54
  233.3 2.6 pad_maximum_fusion
  236.0 10.2 %all_to_all.5 = bf16[2,128,2,16,256]{4,3,1,2,0:T(8,128)(2,1)} all-to-all(bf16[2,128,2,16,256]{4,3,1,2,0:T(8,128)(2,1)S(1)} %pad_maximum_fusion), channel_id=1, replica_groups=mesh['tm'=64,'head'=2] {'head'}, dimensions={0} | all-to-all | bytes 8388608 | tf_op jit(solution)/shard_map/all_to_all | solution.py:56
  246.1 7.9 %copy.15 = bf16[128,2,16,2,256]{0,4,3,2,1:T(8,128)(2,1)} copy(bf16[128,2,16,2,256]{4,2,0,1,3:T(8,128)(2,1)} %bitcast.50) | data formatting | bytes 8388608 | tf_op jit(solution)/shard_map/reshape | solution.py:55
  254.0 2.5 slice_bitcast_fusion.1
  256.5 8.1 %fusion = bf16[16,1024,512]{1,2,0:T(8,128)(2,1)} fusion(bf16[128,16,512]{0,2,1:T(8,128)(2,1)S(1)} %get-tuple-element.6, bf16[128,16,512]{0,2,1:T(8,128)(2,1)S(1)} %get-tuple-element.5, bf16[1024,128]{1,0:T(8,128)(2,1)S(1)} %fusion.11, bf16[1024,128]{1,0:T(8,128)(2,1)S(1)} %cosine_convert_fusion), kind=kOutput, calls=%fused_computation.3 | convolution fusion | flops 4321181696 | bytes 21495808 | tf_op jit(solution)/shard_map/tk,kbf->btf/dot_general | solution.py:59
  264.6 0.0 copy-start.4
  264.6 21.6 %copy.16 = bf16[16,1024,512]{2,1,0:T(8,128)(2,1)} copy(bf16[16,1024,512]{1,2,0:T(8,128)(2,1)} %fusion) | data formatting | bytes 33554432 | tf_op jit(solution)/shard_map/convert_element_type | solution.py:60
  286.3 0.0 copy-done.4
  286.3 0.0 copy-start.1
  286.3 13.7 %convolution_convert_fusion = bf16[16384,256]{1,0:T(8,128)(2,1)} fusion(bf16[16384,512]{1,0:T(8,128)(2,1)} %bitcast.48, bf16[512,256]{1,0:T(8,128)(2,1)S(1)} %copy-done.4), kind=kOutput, calls=%fused_computation.1 | convolution fusion | flops 4299161600 | bytes 25427968 | tf_op jit(solution)/shard_map/dot_general | solution.py:61
  300.0 0.0 copy-done.1
  (4 shorter events, 0.0 us)
Async XLA Ops:
  6.5 1.0 copy-start
  6.5 160.4 %all-reduce.2.cloned.1.call-start = ((), (), s32[]{:S(2)}) async-start(), calls=%async_computation.1 | async-start | bytes 8388608 | tf_op jit(solution)/shard_map/psum | solution.py:37
  7.5 10.3 %copy-start.3 = (s32[128]{0:T(128)S(1)}, s32[128]{0:T(128)}, u32[]{:S(2)}) copy-start(s32[128]{0:T(128)} %param.6) | copy-start | bytes 1540
  26.2 141.9 %copy-start.2 = (f32[2,4,64,128]{3,2,1,0:T(8,128)S(1)}, f32[2,4,64,128]{3,2,1,0:T(8,128)}, u32[]{:S(2)}) copy-start(f32[2,4,64,128]{3,2,1,0:T(8,128)} %param.8) | copy-start | bytes 786436
  26.3 207.1 %all-gather.2.cloned.1.call-start = ((), (), s32[]{:S(2)}) async-start(), calls=%async_computation.2 | async-start | bytes 2129920 | tf_op jit(solution)/shard_map/all_gather | solution.py:54
  264.6 21.6 %copy-start.4 = (bf16[512,256]{1,0:T(8,128)(2,1)S(1)}, bf16[512,256]{1,0:T(8,128)(2,1)}, u32[]{:S(2)}) copy-start(bf16[512,256]{1,0:T(8,128)(2,1)} %param.9) | copy-start | bytes 786436
  286.3 13.7 %copy-start.1 = (bf16[512,256]{1,0:T(8,128)(2,1)S(1)}, bf16[512,256]{1,0:T(8,128)(2,1)}, u32[]{:S(2)}) copy-start(bf16[512,256]{1,0:T(8,128)(2,1)} %param.7) | copy-start | bytes 786436
Sparse Core Ops, SparseCore 0:
  26.4 140.5 all-reduce.1
  170.3 62.9 all-gather.1
